TPU v7x, 32 devices: a whole 2x2x4 slice. The times are simulated.
32 devices in a mesh: fsdp: 2 (over x), ctx: 4 (over y, core), tp: 4 (over z).
Axes of the slice: x: 2, y: 2, z: 4, core: 2. Of those that a mesh axis runs over, the one named last changes fastest.
Arguments:
- tokens: bfloat16 [8, 512, 768], P(('fsdp', 'tp'), 'ctx'), may hold values from -6 to 6
- seg_ids: int32 [8, 512], P(('fsdp', 'tp')), may hold values from 0 to 2, never falling along the last dimension, each value on 1 to 384 neighbouring positions
- routes: int32 [8, 512, 2], P(('fsdp', 'tp'), 'ctx'), may hold values from 0 to 3, all different within a row; in each aligned block of 128 rows (0 to 127, 128 to 255, ..., all dimensions but the last counted through in order) at most 80 rows name the same one
- norm_attn: bfloat16 [768], P('fsdp'), may hold values from 0.5 to 1.5
- weight_qkv: bfloat16 [768, 2304], P('fsdp'), may hold values from -0.21875 to 0.21875
- weight_proj: bfloat16 [768, 768], P(None, 'fsdp'), may hold values from -0.875 to 0.875
- rel_table: float32 [12, 32], replicated, may hold values from -4 to 4
- norm_ffn: bfloat16 [768], P('fsdp'), may hold values from 0.5 to 1.5
- weight_router: bfloat16 [768, 4], P('fsdp'), may hold values from -0.21875 to 0.21875
- expert_up: bfloat16 [4, 768, 3072], P(None, 'fsdp', ('ctx', 'tp')), may hold values from -0.21875 to 0.21875
- expert_down: bfloat16 [4, 3072, 768], P(None, ('ctx', 'tp'), 'fsdp'), may hold values from -0.109375 to 0.109375
- cotangent: bfloat16 [8, 512, 768], P(('fsdp', 'tp'), 'ctx'), may hold values from -6 to 6
Outputs:
- output: bfloat16 [8, 512, 768], P(('fsdp', 'tp'), 'ctx')
- grad_tokens: float32 [8, 512, 768], P(('fsdp', 'tp'), 'ctx')
- grad_norm_attn: float32 [768], P('fsdp')
- grad_weight_qkv: float32 [768, 2304], P('fsdp')
- grad_weight_proj: float32 [768, 768], P(None, 'fsdp')
- grad_rel_table: float32 [12, 32], replicated
- grad_norm_ffn: float32 [768], P('fsdp')
- grad_weight_router: float32 [768, 4], P('fsdp')
- grad_expert_up: float32 [4, 768, 3072], P(None, 'fsdp', ('ctx', 'tp'))
- grad_expert_down: float32 [4, 3072, 768], P(None, ('ctx', 'tp'), 'fsdp')
Inputs may be any that keep to these rules, and one draw needn't show every extreme that they name: `seg_ids`: each group's 512 positions fall into at most 3 sequences whose numbers never fall along the positions; the longest has exactly 384 positions. `routes`: each token names two different experts. In each aligned block of 128 rows (the rows of one device) no expert is named more than 80 times, and in every draw some expert is named exactly 80 times in some block.
All inputs are finite; a program needn't handle non-finite values.
Results may differ from a plain program's by a relative error of at most 0.012.
Values may be sent and summed in bfloat16 or wider, within the bound.
A program may use at most 192 MiB of HBM per device.

v0:
```python
import jax
import jax.numpy as jnp
import numpy as np
from jax import lax
from jax.sharding import PartitionSpec as P

BUCKETS = 32
MAX_DISTANCE = 128
MOST = 80
EPSILON = 1e-06
MASK_FILL = -1e30


def bucket_bounds(buckets, far_reach):
    exact_count = buckets // 2
    bounds = []
    for number in range(1, buckets):
        if number <= exact_count:
            bounds.append(number)
        else:
            exponent = (number - exact_count) / (buckets - exact_count)
            bounds.append(int(np.ceil(exact_count * (far_reach / exact_count) ** exponent)))
    return np.array(bounds, dtype=np.int32)


def bucket_onehot(length):
    bounds = jnp.asarray(bucket_bounds(BUCKETS, MAX_DISTANCE))
    distance = jnp.arange(length, dtype=jnp.int32)
    which_bucket = jnp.sum((distance[:, None] >= bounds[None, :]).astype(jnp.int32), axis=1)
    return (which_bucket[:, None] == jnp.arange(BUCKETS, dtype=jnp.int32)[None, :]).astype(
        jnp.float32
    )


def spread_diagonals(vectors):
    heads_here, length = vectors.shape
    padded = jnp.concatenate([vectors[:, ::-1], jnp.zeros_like(vectors)], axis=1)
    repeated = jnp.tile(padded, (1, length))
    window = repeated[:, length - 1 : length - 1 + length * (2 * length - 1)]
    return window.reshape(heads_here, length, 2 * length - 1)[:, :, :length]


def slot_tables(route_ids, experts, capacity):
    flat_ids = route_ids.reshape(-1)
    assignments = flat_ids.shape[0]
    member = (flat_ids[:, None] == jnp.arange(experts, dtype=jnp.int32)[None, :]).astype(jnp.int32)
    before = jnp.cumsum(member, axis=0) - member
    slot_index = jnp.sum(before * member, axis=1)
    position = slot_index * experts + flat_ids
    filler = (
        jnp.full((capacity * experts,), assignments, jnp.int32)
        .at[position]
        .set(jnp.arange(assignments, dtype=jnp.int32))
    )
    return (position, filler)


def rms_scale(values):
    return lax.rsqrt(jnp.mean(values * values, axis=-1, keepdims=True) + EPSILON)


def local(
    tokens,
    seg_ids,
    routes,
    norm_attn,
    weight_qkv,
    weight_proj,
    rel_table,
    norm_ffn,
    weight_router,
    expert_up,
    expert_down,
    cotangent,
):
    row_count = tokens.shape[1]
    model_width = tokens.shape[2]
    head_count = rel_table.shape[0]
    head_size = model_width // head_count
    heads_here = head_count // lax.axis_size("ctx")
    expert_count = expert_up.shape[0]
    length = seg_ids.shape[1]
    score_scale = head_size ** (-0.5)
    ctx_index = lax.axis_index("ctx")
    head_width = heads_here * head_size
    gathered = (
        lax.all_gather(norm_attn, "fsdp", axis=0, tiled=True),
        lax.all_gather(weight_qkv, "fsdp", axis=0, tiled=True),
        lax.all_gather(weight_proj, "fsdp", axis=1, tiled=True),
        lax.all_gather(weight_router, "fsdp", axis=0, tiled=True),
        lax.all_gather(norm_ffn, "fsdp", axis=0, tiled=True),
        lax.all_gather(expert_up, "fsdp", axis=1, tiled=True),
        lax.all_gather(expert_down, "fsdp", axis=2, tiled=True),
    )
    gain_one, qkv_full, proj_full, router_full, gain_two, up_full, down_full = gathered
    inputs = tokens[0].astype(jnp.float32)
    scale_one = rms_scale(inputs)
    normed_one = (inputs * scale_one * gain_one.astype(jnp.float32)).astype(jnp.bfloat16)
    projected = jnp.dot(normed_one, qkv_full, preferred_element_type=jnp.float32).astype(
        jnp.bfloat16
    )
    by_head = lax.all_to_all(
        projected.reshape(row_count, 3, head_count, head_size),
        "ctx",
        split_axis=2,
        concat_axis=0,
        tiled=True,
    )
    query_rows = by_head[:, 0]
    key_rows = by_head[:, 1]
    value_rows = by_head[:, 2]
    table_here = lax.dynamic_slice_in_dim(rel_table, ctx_index * heads_here, heads_here, 0)
    onehot = bucket_onehot(length)
    bias_vector = jnp.dot(table_here, onehot.T, precision=lax.Precision.HIGHEST)
    bias_matrix = spread_diagonals(bias_vector)
    positions = jnp.arange(length, dtype=jnp.int32)
    segment = seg_ids[0]
    allowed = (segment[:, None] == segment[None, :]) & (positions[:, None] >= positions[None, :])
    block_count = length // length
    query_blocks = query_rows.reshape(block_count, length, heads_here, head_size)
    bias_blocks = jnp.moveaxis(bias_matrix.reshape(heads_here, block_count, length, length), 1, 0)
    mask_blocks = allowed.reshape(block_count, length, length)

    def block_scores(query_block, bias_block, mask_block):
        products = jnp.einsum(
            "qhd,khd->hqk", query_block, key_rows, preferred_element_type=jnp.float32
        )
        return jnp.where(mask_block[None], products * score_scale + bias_block, MASK_FILL)

    def forward_block(pieces):
        query_block, bias_block, mask_block = pieces
        scores = block_scores(query_block, bias_block, mask_block)
        row_peak = jnp.max(scores, axis=-1, keepdims=True)
        weights = jnp.exp(scores - row_peak)
        row_total = jnp.sum(weights, axis=-1, keepdims=True)
        low_probs = (weights / row_total).astype(jnp.bfloat16)
        attended = jnp.einsum(
            "hqk,khd->qhd", low_probs, value_rows, preferred_element_type=jnp.float32
        ).astype(jnp.bfloat16)
        return (attended, (row_peak + jnp.log(row_total))[..., 0])

    attended_blocks, log_totals = lax.map(forward_block, (query_blocks, bias_blocks, mask_blocks))
    attended_heads = attended_blocks.reshape(length, heads_here, head_size)
    back_tokens = lax.all_to_all(attended_heads, "ctx", split_axis=0, concat_axis=1, tiled=True)
    mixed_heads = back_tokens.reshape(row_count, model_width)
    attention = jnp.dot(mixed_heads, proj_full, preferred_element_type=jnp.float32)
    middle = inputs + attention
    scale_two = rms_scale(middle)
    normed_two = (middle * scale_two * gain_two.astype(jnp.float32)).astype(jnp.bfloat16)
    logits = jnp.dot(normed_two, router_full, preferred_element_type=jnp.float32)
    route_ids = routes[0]
    choose = (
        route_ids[:, :, None] == jnp.arange(expert_count, dtype=jnp.int32)[None, None, :]
    ).astype(jnp.float32)
    picked = jnp.sum(choose * logits[:, None, :], axis=2)
    gate_raw = jnp.exp(picked - jnp.max(picked, axis=1, keepdims=True))
    gate_weights = gate_raw / jnp.sum(gate_raw, axis=1, keepdims=True)
    position, filler = slot_tables(route_ids, expert_count, MOST)
    padded_rows = jnp.concatenate([normed_two, jnp.zeros((1, model_width), jnp.bfloat16)], axis=0)
    dispatched = padded_rows[filler // 2].reshape(MOST, expert_count, model_width)
    arrived = lax.all_gather(dispatched, ("ctx", "tp"), axis=0, tiled=True)
    pre_act = jnp.einsum("sed,edf->sef", arrived, up_full, preferred_element_type=jnp.float32)
    activated = jax.nn.gelu(pre_act).astype(jnp.bfloat16)
    row_block = activated
    expert_result = lax.psum_scatter(
        jnp.einsum("sef,efd->sed", row_block, down_full, preferred_element_type=jnp.float32),
        ("ctx", "tp"),
        scatter_dimension=0,
        tiled=True,
    )
    per_choice = expert_result.reshape(MOST * expert_count, model_width)[position].reshape(
        row_count, 2, model_width
    )
    result = middle + jnp.sum(gate_weights[:, :, None] * per_choice, axis=1)
    output = result.astype(jnp.bfloat16)[None]
    again = (
        lax.all_gather(norm_attn, "fsdp", axis=0, tiled=True),
        lax.all_gather(weight_qkv, "fsdp", axis=0, tiled=True),
        lax.all_gather(weight_proj, "fsdp", axis=1, tiled=True),
        lax.all_gather(weight_router, "fsdp", axis=0, tiled=True),
        lax.all_gather(norm_ffn, "fsdp", axis=0, tiled=True),
        lax.all_gather(expert_up, "fsdp", axis=1, tiled=True),
        lax.all_gather(expert_down, "fsdp", axis=2, tiled=True),
    )
    gain_first, qkv_again, proj_again, router_again, gain_second, up_again, down_again = again
    grad_out = cotangent[0].astype(jnp.float32)
    gate_dots = jnp.sum(grad_out[:, None, :] * per_choice, axis=2)
    grad_pick = gate_weights * (
        gate_dots - jnp.sum(gate_weights * gate_dots, axis=1, keepdims=True)
    )
    grad_logits = jnp.sum(grad_pick[:, :, None] * choose, axis=1)
    grad_choice = (
        (gate_weights[:, :, None] * grad_out[:, None, :])
        .astype(jnp.bfloat16)
        .reshape(2 * row_count, model_width)
    )
    padded_grads = jnp.concatenate([grad_choice, jnp.zeros((1, model_width), jnp.bfloat16)], axis=0)
    grad_slots = padded_grads[filler].reshape(MOST, expert_count, model_width)
    grad_arrived = lax.all_gather(grad_slots, ("ctx", "tp"), axis=0, tiled=True)
    grad_act = jnp.einsum(
        "sed,efd->sef", grad_arrived, down_again, preferred_element_type=jnp.float32
    )
    grad_down = jnp.einsum(
        "sef,sed->efd", activated, grad_arrived, preferred_element_type=jnp.float32
    )
    gelu_back = jax.vjp(jax.nn.gelu, pre_act)[1]
    grad_pre = gelu_back(grad_act)[0].astype(jnp.bfloat16)
    grad_up = jnp.einsum("sed,sef->edf", arrived, grad_pre, preferred_element_type=jnp.float32)
    row_block = grad_pre
    grad_dispatched = lax.psum_scatter(
        jnp.einsum("sef,edf->sed", row_block, up_again, preferred_element_type=jnp.float32),
        ("ctx", "tp"),
        scatter_dimension=0,
        tiled=True,
    )
    grad_normed_two = jnp.sum(
        grad_dispatched.reshape(MOST * expert_count, model_width)[position].reshape(
            row_count, 2, model_width
        ),
        axis=1,
    )
    router_float = router_again.astype(jnp.float32)
    grad_normed_two = grad_normed_two + jnp.dot(
        grad_logits, router_float.T, precision=lax.Precision.HIGHEST
    )
    grad_router = jnp.dot(
        normed_two.astype(jnp.float32).T, grad_logits, precision=lax.Precision.HIGHEST
    )
    weighted_two = grad_normed_two * gain_second.astype(jnp.float32)
    grad_gain_two = jnp.sum(grad_normed_two * middle * scale_two, axis=0)
    grad_middle = (
        grad_out
        + scale_two * weighted_two
        - middle * scale_two**3 * jnp.mean(weighted_two * middle, axis=1, keepdims=True)
    )
    grad_middle_low = grad_middle.astype(jnp.bfloat16)
    normed_group, grad_mid_group = (
        lax.all_gather(normed_one, "ctx", axis=0, tiled=True),
        lax.all_gather(grad_middle_low, "ctx", axis=0, tiled=True),
    )
    proj_rows = lax.dynamic_slice_in_dim(proj_again, ctx_index * head_width, head_width, 0)
    grad_attended = jnp.einsum(
        "te,de->td", grad_mid_group, proj_rows, preferred_element_type=jnp.float32
    ).astype(jnp.bfloat16)
    grad_proj_part = jnp.einsum(
        "td,te->de",
        attended_heads.reshape(length, head_width),
        grad_mid_group,
        preferred_element_type=jnp.float32,
    )
    grad_blocks = grad_attended.reshape(block_count, length, heads_here, head_size)

    def backward_block(running, pieces):
        key_sum, value_sum = running
        query_block, bias_block, mask_block, log_block, grad_block = pieces
        scores = block_scores(query_block, bias_block, mask_block)
        probs_float = jnp.exp(scores - log_block[..., None])
        low_probs = probs_float.astype(jnp.bfloat16)
        value_term = jnp.einsum(
            "hqk,qhd->khd", low_probs, grad_block, preferred_element_type=jnp.float32
        )
        grad_probs = jnp.einsum(
            "qhd,khd->hqk", grad_block, value_rows, preferred_element_type=jnp.float32
        )
        grad_scores = (
            probs_float * (grad_probs - jnp.sum(probs_float * grad_probs, axis=-1, keepdims=True))
        ).astype(jnp.bfloat16)
        query_term = (
            jnp.einsum("hqk,khd->qhd", grad_scores, key_rows, preferred_element_type=jnp.float32)
            * score_scale
        ).astype(jnp.bfloat16)
        key_term = (
            jnp.einsum("hqk,qhd->khd", grad_scores, query_block, preferred_element_type=jnp.float32)
            * score_scale
        )
        return ((key_sum + key_term, value_sum + value_term), (query_term, grad_scores))

    zero_rows = jnp.zeros((length, heads_here, head_size), jnp.float32)
    sums_kv, per_block = lax.scan(
        backward_block,
        (zero_rows, zero_rows),
        (query_blocks, bias_blocks, mask_blocks, log_totals, grad_blocks),
    )
    query_grads, score_grads = per_block
    grad_qkv_heads = jnp.stack(
        [
            query_grads.reshape(length, heads_here, head_size),
            sums_kv[0].astype(jnp.bfloat16),
            sums_kv[1].astype(jnp.bfloat16),
        ],
        axis=1,
    )
    grad_qkv_part = jnp.einsum(
        "td,tshk->dshk", normed_group, grad_qkv_heads, preferred_element_type=jnp.float32
    )
    grad_projected = lax.all_to_all(
        grad_qkv_heads, "ctx", split_axis=0, concat_axis=2, tiled=True
    ).reshape(row_count, 3 * model_width)
    score_matrix = (
        jnp.moveaxis(score_grads, 0, 1).reshape(heads_here, length, length).astype(jnp.float32)
    )
    spread_back = jax.vjp(spread_diagonals, bias_vector)[1]
    grad_vector = spread_back(score_matrix)[0]
    grad_table_here = jnp.dot(grad_vector, onehot, precision=lax.Precision.HIGHEST)
    table_term = lax.dynamic_update_slice_in_dim(
        jnp.zeros((head_count, BUCKETS), jnp.float32), grad_table_here, ctx_index * heads_here, 0
    )
    grad_normed_one = jnp.einsum(
        "te,de->td", grad_projected, qkv_again, preferred_element_type=jnp.float32
    )
    weighted_one = grad_normed_one * gain_first.astype(jnp.float32)
    grad_gain_one = jnp.sum(grad_normed_one * inputs * scale_one, axis=0)
    grad_tokens = (
        grad_middle
        + scale_one * weighted_one
        - inputs * scale_one**3 * jnp.mean(weighted_one * inputs, axis=1, keepdims=True)
    )
    shares = (
        lax.psum_scatter(grad_gain_one, "fsdp", scatter_dimension=0, tiled=True),
        lax.psum_scatter(grad_qkv_part, "fsdp", scatter_dimension=0, tiled=True),
        lax.psum_scatter(grad_proj_part, "fsdp", scatter_dimension=1, tiled=True),
        lax.psum_scatter(grad_router, "fsdp", scatter_dimension=0, tiled=True),
        lax.psum_scatter(grad_gain_two, "fsdp", scatter_dimension=0, tiled=True),
        lax.psum_scatter(grad_up, "fsdp", scatter_dimension=1, tiled=True),
        lax.psum_scatter(grad_down, "fsdp", scatter_dimension=2, tiled=True),
    )
    qkv_share = shares[1]
    own_rows = qkv_share.shape[0]
    qkv_placed = lax.dynamic_update_slice_in_dim(
        jnp.zeros((own_rows, 3, head_count, head_size), jnp.float32),
        qkv_share,
        ctx_index * heads_here,
        2,
    ).reshape(own_rows, 3 * model_width)
    proj_share = shares[2]
    proj_placed = lax.dynamic_update_slice_in_dim(
        jnp.zeros((model_width, proj_share.shape[1]), jnp.float32),
        proj_share,
        ctx_index * head_width,
        0,
    )
    summed = lax.psum((shares[0], qkv_placed, proj_placed, shares[3], shares[4]), ("ctx", "tp"))
    table_grad = lax.psum(table_term, ("fsdp", "ctx", "tp"))
    return (
        output,
        grad_tokens[None],
        summed[0],
        summed[1],
        summed[2],
        table_grad,
        summed[4],
        summed[3],
        shares[5],
        shares[6],
    )


def solution(mesh):
    in_specs = (
        P(("fsdp", "tp"), "ctx", None),
        P(("fsdp", "tp"), None),
        P(("fsdp", "tp"), "ctx", None),
        P("fsdp"),
        P("fsdp", None),
        P(None, "fsdp"),
        P(),
        P("fsdp"),
        P("fsdp", None),
        P(None, "fsdp", ("ctx", "tp")),
        P(None, ("ctx", "tp"), "fsdp"),
        P(("fsdp", "tp"), "ctx", None),
    )
    out_specs = (
        P(("fsdp", "tp"), "ctx", None),
        P(("fsdp", "tp"), "ctx", None),
        P("fsdp"),
        P("fsdp", None),
        P(None, "fsdp"),
        P(),
        P("fsdp"),
        P("fsdp", None),
        P(None, "fsdp", ("ctx", "tp")),
        P(None, ("ctx", "tp"), "fsdp"),
    )
    return jax.shard_map(local, mesh=mesh, in_specs=in_specs, out_specs=out_specs, check_vma=False)
```

profile of v0, /device:TPU:0, one launch (start us, length us, event | category | flops | bytes accessed | tf_op | source)
XLA Modules:
  0.0 897.2 jit_solution(6429418993881922095)
XLA Ops:
  27.6 7.1 copy.178
  34.7 6.6 slice.39
  41.3 13.2 %reshape.303 = f32[3,512,1023]{2,1,0:T(8,128)} reshape(f32[3,523776]{1,0:T(4,128)} %slice.39) | data formatting | bytes 12570624 | tf_op jit(solution)/shard_map/reshape | solution.py:40
  70.7 8.0 all-to-all-done
  140.9 44.0 %all-gather.13.cloned.1.call-done = bf16[1280,4,768]{2,0,1:T(8,128)(2,1)} async-done(((bf16[80,4,768]{2,0,1:T(8,128)(2,1)}), bf16[1280,4,768]{2,0,1:T(8,128)(2,1)}) %all-gather.13.cloned.1.call-update) | async-done | bytes 7864336 | tf_op jit(solution)/shard_map/all_gather | solution.py:161
  184.9 8.1 fusion.63
  193.0 14.4 %all-gather.17.cloned.1.call-done = bf16[4,192,768]{2,1,0:T(8,128)(2,1)} async-done(((bf16[4,192,384]{2,1,0:T(8,128)(2,1)}), bf16[4,192,768]{2,1,0:T(8,128)(2,1)}) %all-gather.17.cloned.1.call-update) | async-done | bytes 1179664 | tf_op jit(solution)/shard_map/all_gather | solution.py:93
  207.5 10.3 %convolution_bitcast_fusion.1 = f32[1280,4,768]{2,0,1:T(8,128)} fusion(bf16[4,192,768]{2,1,0:T(8,128)(2,1)} %all-gather.17.cloned.1.call-done, f32[4,1280,192]{1,2,0:T(8,128)} %fusion.63), kind=kOutput, calls=%fused_computation.6 | convolution fusion | flops 1518796800 | bytes 20840448 | tf_op jit(solution)/shard_map/sef,efd->sed/dot_general | solution.py:166
  218.0 63.8 %all-gather.19.cloned.1.call-done = bf16[1280,4,768]{2,0,1:T(8,128)(2,1)} async-done(((bf16[80,4,768]{2,0,1:T(8,128)(2,1)}), bf16[1280,4,768]{2,0,1:T(8,128)(2,1)}) %all-gather.19.cloned.1.call-update) | async-done | bytes 7864336 | tf_op jit(solution)/shard_map/all_gather | solution.py:199
  281.9 8.6 fusion.6
  291.7 10.6 %convolution_bitcast_fusion = f32[1280,4,768]{2,0,1:T(8,128)} fusion(bf16[1280,4,192]{0,2,1:T(8,128)(2,1)S(1)} %fusion.6, bf16[4,768,192]{1,2,0:T(8,128)(2,1)S(1)} %copy-done.7), kind=kOutput, calls=%fused_computation.5 | convolution fusion | flops 1509949440 | bytes 18874368 | tf_op jit(solution)/shard_map/sef,edf->sed/dot_general | solution.py:211
  303.6 9.7 %all_gather.50 = bf16[512,768]{1,0:T(8,128)(2,1)} all-gather(bf16[128,768]{1,0:T(8,128)(2,1)} %copy-done.19), channel_id=1, replica_groups=mesh['fsdp'=2,'ctx'=4,'tp'=4] {'ctx'}, dimensions={0}, use_global_device_ids=true | all-gather | bytes 983040 | tf_op jit(solution)/shard_map/all_gather | solution.py:238
  314.0 127.2 %reduce-scatter.10.cloned.1.call-done = f32[80,4,768]{2,0,1:T(8,128)} async-done(((f32[1280,4,768]{2,0,1:T(8,128)}), f32[80,4,768]{2,0,1:T(8,128)}) %reduce-scatter.10.cloned.1.call-update) | async-done | bytes 983056 | tf_op jit(solution)/shard_map/reduce_scatter | solution.py:165
  459.1 142.7 %reduce-scatter.12.cloned.1.call-done = f32[80,4,768]{2,0,1:T(8,128)} async-done(((f32[1280,4,768]{2,0,1:T(8,128)}), f32[80,4,768]{2,0,1:T(8,128)}) %reduce-scatter.12.cloned.1.call-update) | async-done | bytes 983056 | tf_op jit(solution)/shard_map/reduce_scatter | solution.py:210
  620.4 8.6 all_gather.49
  648.1 28.3 %reduce-scatter.14.cloned.1.call-done = f32[384,3,3,64]{0,3,2,1:T(8,128)} async-done(((f32[768,3,3,64]{0,3,2,1:T(8,128)}), f32[384,3,3,64]{0,3,2,1:T(8,128)}) %reduce-scatter.14.cloned.1.call-update) | async-done | bytes 884752 | tf_op jit(solution)/shard_map/reduce_scatter | solution.py:320
  679.5 7.0 fusion.67
  688.0 7.8 fusion.57
  703.2 7.6 reshape.380
  710.9 5.7 reshape.314
  734.8 39.7 %psum.45 = f32[12,32]{1,0:T(8,128)} all-reduce(f32[12,32]{1,0:T(8,128)S(1)} %dynamic_update_slice.22), channel_id=1, replica_groups=mesh['fsdp'=2,'ctx'=4,'tp'=4] {'fsdp','ctx','tp'}, use_global_device_ids=true, to_apply=%region_30.31 | all-reduce | flops 384 | bytes 3072 | tf_op jit(solution)/shard_map/psum | solution.py:343
  786.7 5.3 all-reduce.9
  792.1 60.5 %all-reduce.7 = (f32[384]{0:T(512)}, f32[384]{0:T(512)}, f32[384,4]{0,1:T(4,128)}) all-reduce(f32[384]{0:T(512)S(1)} %dynamic-slice.3, f32[384]{0:T(512)S(1)} %dynamic-slice.5, f32[384,4]{0,1:T(4,128)S(1)} %copy.175), channel_id=1, replica_groups=mesh['fsdp'=2,'ctx'=4,'tp'=4] {'ctx','tp'}, use_global_device_ids=true, to_apply=%region_24.25 | all-reduce | flops 2304 | bytes 18432 | tf_op jit(solution)/shard_map/psum | solution.py:342
  860.6 28.8 %reduce-scatter.20.cloned.1.call-done = f32[4,192,384]{2,1,0:T(8,128)} async-done(((f32[4,192,768]{2,1,0:T(8,128)}), f32[4,192,384]{2,1,0:T(8,128)}) %reduce-scatter.20.cloned.1.call-update) | async-done | bytes 1179664 | tf_op jit(solution)/shard_map/reduce_scatter | solution.py:325
  (259 shorter events, 208.3 us)
Async XLA Ops:
  7.2 54.5 %all-gather.9.cloned.1.call-start = ((), (), s32[]{:S(2)}) async-start(), calls=%async_computation.10 | async-start | bytes 5308416 | tf_op jit(solution)/shard_map/all_gather | solution.py:88
  8.0 93.8 %all-gather.11.cloned.1.call-start = ((), (), s32[]{:S(2)}) async-start(), calls=%async_computation.11 | async-start | bytes 1769472 | tf_op jit(solution)/shard_map/all_gather | solution.py:89
  8.7 132.2 %all-gather.15.cloned.1.call-start = ((), (), s32[]{:S(2)}) async-start(), calls=%async_computation.13 | async-start | bytes 1769472 | tf_op jit(solution)/shard_map/all_gather | solution.py:92
  11.4 47.3 %copy-start.36 = (f32[128]{0:T(128)}, f32[128]{0:T(128)S(1)}, u32[]{:S(2)}) copy-start(f32[128]{0:T(128)S(1)} %get-tuple-element.139) | copy-start | bytes 1540
  16.7 42.1 %copy-start.26 = (f32[768]{0:T(1024)}, f32[768]{0:T(1024)S(1)}, u32[]{:S(2)}) copy-start(f32[768]{0:T(1024)S(1)} %reshape.367) | copy-start | bytes 9220
  65.6 13.2 %all-to-all-start = ((bf16[128,3,12,64]{0,3,1,2:T(8,128)(2,1)}), bf16[128,3,12,64]{0,3,1,2:T(8,128)(2,1)S(1)}, u32[]{:S(2)}, u32[]{:S(2)}) async-start(bf16[128,3,12,64]{0,3,1,2:T(8,128)(2,1)} %copy.136), calls=%async_computation | async-start | bytes 1179648 | tf_op jit(solution)/shard_map/all_to_all | solution.py:102
  85.3 18.9 %copy-start.22 = (bf16[3,64,512]{2,1,0:T(8,128)(2,1)}, bf16[3,64,512]{2,1,0:T(8,128)(2,1)S(1)}, u32[]{:S(2)}) copy-start(bf16[3,64,512]{2,1,0:T(8,128)(2,1)S(1)} %fusion.19) | copy-start | bytes 589828
  88.4 9.4 %all-to-all-start.1 = ((bf16[4,2,12288]{2,1,0:T(2,128)(2,1)}), bf16[4,2,12288]{2,1,0:T(2,128)(2,1)}, u32[]{:S(2)}, u32[]{:S(2)}) async-start(bf16[4,2,12288]{2,1,0:T(2,128)(2,1)} %reshape.382), calls=%async_computation.1 | async-start | bytes 393216 | tf_op jit(solution)/shard_map/all_to_all | solution.py:144
  92.4 92.5 %all-gather.13.cloned.1.call-start = ((), (), s32[]{:S(2)}) async-start(), calls=%async_computation.12 | async-start | bytes 8355840 | tf_op jit(solution)/shard_map/all_gather | solution.py:161
  112.0 95.5 %all-gather.17.cloned.1.call-start = ((), (), s32[]{:S(2)}) async-start(), calls=%async_computation.14 | async-start | bytes 1769472 | tf_op jit(solution)/shard_map/all_gather | solution.py:93
  112.6 169.3 %all-gather.19.cloned.1.call-start = ((), (), s32[]{:S(2)}) async-start(), calls=%async_computation.16 | async-start | bytes 8355840 | tf_op jit(solution)/shard_map/all_gather | solution.py:199
  140.9 300.3 %reduce-scatter.10.cloned.1.call-start = ((), (), s32[]{:S(2)}) async-start(), calls=%async_computation.15 | async-start | bytes 16711680 | tf_op jit(solution)/shard_map/reduce_scatter | solution.py:165
  217.8 384.0 %reduce-scatter.12.cloned.1.call-start = ((), (), s32[]{:S(2)}) async-start(), calls=%async_computation.17 | async-start | bytes 16711680 | tf_op jit(solution)/shard_map/reduce_scatter | solution.py:210
  302.3 343.0 %reduce-scatter.16.cloned.1.call-start = ((), (), s32[]{:S(2)}) async-start(), calls=%async_computation.19 | async-start | bytes 884736 | tf_op jit(solution)/shard_map/reduce_scatter | solution.py:321
  631.0 45.4 %reduce-scatter.14.cloned.1.call-start = ((), (), s32[]{:S(2)}) async-start(), calls=%async_computation.18 | async-start | bytes 2654208 | tf_op jit(solution)/shard_map/reduce_scatter | solution.py:320
  640.2 134.3 %reduce-scatter.22.cloned.1.call-start = ((), (), s32[]{:S(2)}) async-start(), calls=%async_computation.22 | async-start | bytes 589824
  641.4 214.0 %all-reduce.12.cloned.1.call-start = ((), (), s32[]{:S(2)}) async-start(), calls=%async_computation.23 | async-start | bytes 9437184 | tf_op jit(solution)/shard_map/psum | solution.py:342
  679.5 181.2 %reduce-scatter.18.cloned.1.call-start = ((), (), s32[]{:S(2)}) async-start(), calls=%async_computation.20 | async-start | bytes 3538944 | tf_op jit(solution)/shard_map/reduce_scatter | solution.py:324
  686.5 202.9 %reduce-scatter.20.cloned.1.call-start = ((), (), s32[]{:S(2)}) async-start(), calls=%async_computation.21 | async-start | bytes 3538944 | tf_op jit(solution)/shard_map/reduce_scatter | solution.py:325
  718.7 56.8 %all-to-all-start.2 = ((bf16[4,2,36864]{2,1,0:T(2,128)(2,1)}), bf16[4,2,36864]{2,1,0:T(2,128)(2,1)}, u32[]{:S(2)}, u32[]{:S(2)}) async-start(bf16[4,2,36864]{2,1,0:T(2,128)(2,1)} %reshape.384), calls=%async_computation.4 | async-start | bytes 1179648 | tf_op jit(solution)/shard_map/all_to_all | solution.py:296
  731.0 51.8 %copy-start.4 = (bf16[768,2304]{1,0:T(8,128)(2,1)S(1)}, bf16[768,2304]{1,0:T(8,128)(2,1)}, u32[]{:S(2)}) copy-start(bf16[768,2304]{1,0:T(8,128)(2,1)} %all-gather.9.cloned.1.call-done) | copy-start | bytes 10616836
  731.0 51.8 %copy-start.27 = (f32[768]{0:T(1024)S(1)}, f32[768]{0:T(1024)}, u32[]{:S(2)}) copy-start(f32[768]{0:T(1024)} %copy-done.26) | copy-start | bytes 9220
  855.4 35.1 %copy-start.1 = (f32[12,32]{1,0:T(8,128)S(1)}, f32[12,32]{1,0:T(8,128)}, u32[]{:S(2)}) copy-start(f32[12,32]{1,0:T(8,128)} %param.19) | copy-start | bytes 4612
  855.4 34.1 %copy-start.20 = (f32[768,384]{1,0:T(8,128)S(1)}, f32[768,384]{1,0:T(8,128)}, u32[]{:S(2)}) copy-start(f32[768,384]{1,0:T(8,128)} %get-tuple-element.156) | copy-start | bytes 3538948
  (39 other events, 194.2 us)
Sparse Core Ops, SparseCore 0:
  9.6 52.0 all-gather.8
  63.3 22.7 all-gather.10
  87.7 22.7 all-gather.14
  113.3 71.5 all-gather.12
  186.3 21.1 all-gather.16
  210.2 71.5 all-gather.18
  286.0 155.1 reduce-scatter.9
  445.8 155.9 reduce-scatter.11
  631.1 14.1 reduce-scatter.15
  648.1 28.2 reduce-scatter.13
  678.6 13.0 reduce-scatter.21
  696.3 118.0 all-reduce.11
  817.3 34.6 reduce-scatter.17
  854.7 34.7 reduce-scatter.19
where the time goes:
time: 905 us; the launch traced here: 897 us
  waiting for transfers between devices  468 us (52%)
  local copies, waits for them, and re-layouts  146 us (16%)
  blocking collectives  138 us (15%)
  matrix products  79.4 us (9%)
  other arithmetic  37 us (4%)
  between operations  15.4 us (2%)
  starting transfers between devices  13.4 us (1%)
    reduce_scatter x1, waiting for transfers between devices, local(): lax.psum_scatter(jnp.einsum('sef,edf->sed', row_block, up_again, preferre...  143 us
    reduce_scatter x1, waiting for transfers between devices, local(): lax.psum_scatter(jnp.einsum('sef,efd->sed', row_block, down_full, preferr...  127 us
    all_gather x1, waiting for transfers between devices, local(): grad_arrived = lax.all_gather(grad_slots, ('ctx', 'tp'), axis=0, tiled=True)  63.8 us
    psum x1, blocking collectives, local(): lax.psum((shares[0], qkv_placed, proj_placed, shares[3], shares[4]), ('ct...  60.5 us
    unnamed x108, local copies, waits for them, and re-layouts  51.7 us
    all_gather x1, waiting for transfers between devices, local(): arrived = lax.all_gather(dispatched, ('ctx', 'tp'), axis=0, tiled=True)  44 us
    psum x1, blocking collectives, local(): table_grad = lax.psum(table_term, ('fsdp', 'ctx', 'tp'))  39.7 us
    reduce_scatter x1, waiting for transfers between devices, local(): lax.psum_scatter(grad_down, 'fsdp', scatter_dimension=2, tiled=True)  28.8 us
  transfers between devices with their start and end apart: 17, of which 11 were waited for; matrix products, arithmetic and copies ran while one was open for 25% of the time, Pallas kernels for 0%

commit v1 on v0

--- a/solution.py
+++ b/solution.py
@@ -340,7 +340,7 @@
         0,
     )
     summed = lax.psum((shares[0], qkv_placed, proj_placed, shares[3], shares[4]), ("ctx", "tp"))
-    table_grad = lax.psum(table_term, ("fsdp", "ctx", "tp"))
+    table_grad = jnp.sum(lax.all_gather(table_term, ("fsdp", "ctx", "tp")), axis=0)
     return (
         output,
         grad_tokens[None],

time: 905 us -> 912 us (level)
  blocking collectives: 138 us -> 172 us
  waiting for transfers between devices: 468 us -> 440 us
    all_gather x0 -> x1, blocking collectives: none -> 76.4 us  [local(): lax.all_gather(table_term, ('fsdp', 'ctx', 'tp'))]
    psum x1 -> x0, blocking collectives: 39.7 us -> none  [local(): table_grad = lax.psum(table_term, ('fsdp', 'ctx', 'tp'))]
    reduce_scatter x1, waiting for transfers between devices: 28.8 us -> 0.01 us  [local(): lax.psum_scatter(grad_down, 'fsdp', scatter_dimension=2, tiled=True)]
  transfers between devices with their start and end apart: 17 -> 17, of which waited for: 11 -> 10; matrix products, arithmetic and copies ran while one was open for 25% -> 25% of each run, Pallas kernels for 0% -> 0%
where the time goes in v1:
time: 912 us; the launch traced here: 904 us
  waiting for transfers between devices  440 us (48%)
  blocking collectives  172 us (19%)
  local copies, waits for them, and re-layouts  146 us (16%)
  matrix products  79.3 us (9%)
  other arithmetic  38.6 us (4%)
  between operations  15.4 us (2%)
  starting transfers between devices  13.7 us (2%)
    reduce_scatter x1, waiting for transfers between devices, local(): lax.psum_scatter(jnp.einsum('sef,edf->sed', row_block, up_again, preferre...  143 us
    reduce_scatter x1, waiting for transfers between devices, local(): lax.psum_scatter(jnp.einsum('sef,efd->sed', row_block, down_full, preferr...  127 us
    all_gather x1, blocking collectives, local(): lax.all_gather(table_term, ('fsdp', 'ctx', 'tp'))  76.4 us
    all_gather x1, waiting for transfers between devices, local(): grad_arrived = lax.all_gather(grad_slots, ('ctx', 'tp'), axis=0, tiled=True)  63.9 us
    psum x1, blocking collectives, local(): lax.psum((shares[0], qkv_placed, proj_placed, shares[3], shares[4]), ('ct...  58 us
    unnamed x108, local copies, waits for them, and re-layouts  51.7 us
    all_gather x1, waiting for transfers between devices, local(): arrived = lax.all_gather(dispatched, ('ctx', 'tp'), axis=0, tiled=True)  43.6 us
    reduce_scatter x1, waiting for transfers between devices, local(): lax.psum_scatter(grad_qkv_part, 'fsdp', scatter_dimension=0, tiled=True)  28.4 us
  transfers between devices with their start and end apart: 17, of which 10 were waited for; matrix products, arithmetic and copies ran while one was open for 25% of the time, Pallas kernels for 0%

profile of v1, /device:TPU:0, one launch (start us, length us, event | category | flops | bytes accessed | tf_op | source)
XLA Modules:
  0.0 904.1 jit_solution(570262049001624554)
XLA Ops:
  27.6 7.1 copy.178
  34.7 6.4 slice.39
  41.1 13.2 %reshape.305 = f32[3,512,1023]{2,1,0:T(8,128)} reshape(f32[3,523776]{1,0:T(4,128)} %slice.39) | data formatting | bytes 12570624 | tf_op jit(solution)/shard_map/reshape | solution.py:40
  71.1 8.0 all-to-all-done
  141.3 43.6 %all-gather.13.cloned.1.call-done = bf16[1280,4,768]{2,0,1:T(8,128)(2,1)} async-done(((bf16[80,4,768]{2,0,1:T(8,128)(2,1)}), bf16[1280,4,768]{2,0,1:T(8,128)(2,1)}) %all-gather.13.cloned.1.call-update) | async-done | bytes 7864336 | tf_op jit(solution)/shard_map/all_gather | solution.py:161
  184.9 8.1 fusion.62
  193.0 14.4 %all-gather.17.cloned.1.call-done = bf16[4,192,768]{2,1,0:T(8,128)(2,1)} async-done(((bf16[4,192,384]{2,1,0:T(8,128)(2,1)}), bf16[4,192,768]{2,1,0:T(8,128)(2,1)}) %all-gather.17.cloned.1.call-update) | async-done | bytes 1179664 | tf_op jit(solution)/shard_map/all_gather | solution.py:93
  207.5 10.3 %convolution_bitcast_fusion.1 = f32[1280,4,768]{2,0,1:T(8,128)} fusion(bf16[4,192,768]{2,1,0:T(8,128)(2,1)} %all-gather.17.cloned.1.call-done, f32[4,1280,192]{1,2,0:T(8,128)} %fusion.62), kind=kOutput, calls=%fused_computation.6 | convolution fusion | flops 1518796800 | bytes 20840448 | tf_op jit(solution)/shard_map/sef,efd->sed/dot_general | solution.py:166
  218.0 63.9 %all-gather.19.cloned.1.call-done = bf16[1280,4,768]{2,0,1:T(8,128)(2,1)} async-done(((bf16[80,4,768]{2,0,1:T(8,128)(2,1)}), bf16[1280,4,768]{2,0,1:T(8,128)(2,1)}) %all-gather.19.cloned.1.call-update) | async-done | bytes 7864336 | tf_op jit(solution)/shard_map/all_gather | solution.py:199
  281.9 8.6 fusion.6
  291.7 10.6 %convolution_bitcast_fusion = f32[1280,4,768]{2,0,1:T(8,128)} fusion(bf16[1280,4,192]{0,2,1:T(8,128)(2,1)S(1)} %fusion.6, bf16[4,768,192]{1,2,0:T(8,128)(2,1)S(1)} %copy-done.7), kind=kOutput, calls=%fused_computation.5 | convolution fusion | flops 1509949440 | bytes 18874368 | tf_op jit(solution)/shard_map/sef,edf->sed/dot_general | solution.py:211
  303.6 9.7 %all_gather.56 = bf16[512,768]{1,0:T(8,128)(2,1)} all-gather(bf16[128,768]{1,0:T(8,128)(2,1)} %copy-done.19), channel_id=1, replica_groups=mesh['fsdp'=2,'ctx'=4,'tp'=4] {'ctx'}, dimensions={0}, use_global_device_ids=true | all-gather | bytes 983040 | tf_op jit(solution)/shard_map/all_gather | solution.py:238
  314.0 127.2 %reduce-scatter.10.cloned.1.call-done = f32[80,4,768]{2,0,1:T(8,128)} async-done(((f32[1280,4,768]{2,0,1:T(8,128)}), f32[80,4,768]{2,0,1:T(8,128)}) %reduce-scatter.10.cloned.1.call-update) | async-done | bytes 983056 | tf_op jit(solution)/shard_map/reduce_scatter | solution.py:165
  459.1 142.7 %reduce-scatter.12.cloned.1.call-done = f32[80,4,768]{2,0,1:T(8,128)} async-done(((f32[1280,4,768]{2,0,1:T(8,128)}), f32[80,4,768]{2,0,1:T(8,128)}) %reduce-scatter.12.cloned.1.call-update) | async-done | bytes 983056 | tf_op jit(solution)/shard_map/reduce_scatter | solution.py:210
  620.4 8.6 all_gather.55
  648.1 28.4 %reduce-scatter.14.cloned.1.call-done = f32[384,3,3,64]{0,3,2,1:T(8,128)} async-done(((f32[768,3,3,64]{0,3,2,1:T(8,128)}), f32[384,3,3,64]{0,3,2,1:T(8,128)}) %reduce-scatter.14.cloned.1.call-update) | async-done | bytes 884752 | tf_op jit(solution)/shard_map/reduce_scatter | solution.py:320
  679.6 7.0 fusion.66
  688.3 7.8 fusion.56
  703.4 7.6 reshape.382
  711.0 5.7 reshape.316
  734.9 76.4 %all_gather.58 = f32[32,12,32]{2,1,0:T(8,128)} all-gather(f32[1,12,32]{2,1,0:T(8,128)S(1)} %dynamic_update_slice.23), channel_id=1, replica_groups=mesh['fsdp'=2,'ctx'=4,'tp'=4] {'fsdp','ctx','tp'}, dimensions={0}, use_global_device_ids=true | all-gather | bytes 50688 | tf_op jit(solution)/shard_map/all_gather | solution.py:343
  825.0 5.2 all-reduce.9
  830.4 58.0 %all-reduce.7 = (f32[384]{0:T(512)}, f32[384]{0:T(512)}, f32[384,4]{0,1:T(4,128)}) all-reduce(f32[384]{0:T(512)S(1)} %dynamic-slice.3, f32[384]{0:T(512)S(1)} %dynamic-slice.5, f32[384,4]{0,1:T(4,128)S(1)} %copy.175), channel_id=1, replica_groups=mesh['fsdp'=2,'ctx'=4,'tp'=4] {'ctx','tp'}, use_global_device_ids=true, to_apply=%region_24.25 | all-reduce | flops 2304 | bytes 18432 | tf_op jit(solution)/shard_map/psum | solution.py:342
  891.1 5.2 copy.164
  (260 shorter events, 205.0 us)
Async XLA Ops:
  7.2 54.5 %all-gather.9.cloned.1.call-start = ((), (), s32[]{:S(2)}) async-start(), calls=%async_computation.10 | async-start | bytes 5308416 | tf_op jit(solution)/shard_map/all_gather | solution.py:88
  8.0 94.2 %all-gather.11.cloned.1.call-start = ((), (), s32[]{:S(2)}) async-start(), calls=%async_computation.11 | async-start | bytes 1769472 | tf_op jit(solution)/shard_map/all_gather | solution.py:89
  8.7 132.6 %all-gather.15.cloned.1.call-start = ((), (), s32[]{:S(2)}) async-start(), calls=%async_computation.13 | async-start | bytes 1769472 | tf_op jit(solution)/shard_map/all_gather | solution.py:92
  11.4 47.2 %copy-start.36 = (f32[128]{0:T(128)}, f32[128]{0:T(128)S(1)}, u32[]{:S(2)}) copy-start(f32[128]{0:T(128)S(1)} %get-tuple-element.139) | copy-start | bytes 1540
  16.7 41.9 %copy-start.26 = (f32[768]{0:T(1024)}, f32[768]{0:T(1024)S(1)}, u32[]{:S(2)}) copy-start(f32[768]{0:T(1024)S(1)} %reshape.369) | copy-start | bytes 9220
  65.6 13.5 %all-to-all-start = ((bf16[128,3,12,64]{0,3,1,2:T(8,128)(2,1)}), bf16[128,3,12,64]{0,3,1,2:T(8,128)(2,1)S(1)}, u32[]{:S(2)}, u32[]{:S(2)}) async-start(bf16[128,3,12,64]{0,3,1,2:T(8,128)(2,1)} %copy.136), calls=%async_computation | async-start | bytes 1179648 | tf_op jit(solution)/shard_map/all_to_all | solution.py:102
  85.6 18.9 %copy-start.22 = (bf16[3,64,512]{2,1,0:T(8,128)(2,1)}, bf16[3,64,512]{2,1,0:T(8,128)(2,1)S(1)}, u32[]{:S(2)}) copy-start(bf16[3,64,512]{2,1,0:T(8,128)(2,1)S(1)} %fusion.19) | copy-start | bytes 589828
  88.8 9.4 %all-to-all-start.1 = ((bf16[4,2,12288]{2,1,0:T(2,128)(2,1)}), bf16[4,2,12288]{2,1,0:T(2,128)(2,1)}, u32[]{:S(2)}, u32[]{:S(2)}) async-start(bf16[4,2,12288]{2,1,0:T(2,128)(2,1)} %reshape.384), calls=%async_computation.1 | async-start | bytes 393216 | tf_op jit(solution)/shard_map/all_to_all | solution.py:144
  92.8 92.1 %all-gather.13.cloned.1.call-start = ((), (), s32[]{:S(2)}) async-start(), calls=%async_computation.12 | async-start | bytes 8355840 | tf_op jit(solution)/shard_map/all_gather | solution.py:161
  93.5 15.0 %copy-start.24 = (f32[768]{0:T(1024)}, f32[768]{0:T(1024)S(1)}, u32[]{:S(2)}) copy-start(f32[768]{0:T(1024)S(1)} %reshape.370) | copy-start | bytes 9220
  112.3 95.1 %all-gather.17.cloned.1.call-start = ((), (), s32[]{:S(2)}) async-start(), calls=%async_computation.14 | async-start | bytes 1769472 | tf_op jit(solution)/shard_map/all_gather | solution.py:93
  112.9 168.9 %all-gather.19.cloned.1.call-start = ((), (), s32[]{:S(2)}) async-start(), calls=%async_computation.16 | async-start | bytes 8355840 | tf_op jit(solution)/shard_map/all_gather | solution.py:199
  122.1 15.3 %copy-start.28 = (bf16[768,4]{0,1:T(4,128)(2,1)}, bf16[768,4]{0,1:T(4,128)(2,1)S(1)}, u32[]{:S(2)}) copy-start(bf16[768,4]{0,1:T(4,128)(2,1)S(1)} %all_gather.50) | copy-start | bytes 18436
  141.2 300.0 %reduce-scatter.10.cloned.1.call-start = ((), (), s32[]{:S(2)}) async-start(), calls=%async_computation.15 | async-start | bytes 16711680 | tf_op jit(solution)/shard_map/reduce_scatter | solution.py:165
  217.8 384.0 %reduce-scatter.12.cloned.1.call-start = ((), (), s32[]{:S(2)}) async-start(), calls=%async_computation.17 | async-start | bytes 16711680 | tf_op jit(solution)/shard_map/reduce_scatter | solution.py:210
  302.3 343.0 %reduce-scatter.16.cloned.1.call-start = ((), (), s32[]{:S(2)}) async-start(), calls=%async_computation.19 | async-start | bytes 884736 | tf_op jit(solution)/shard_map/reduce_scatter | solution.py:321
  631.0 45.5 %reduce-scatter.14.cloned.1.call-start = ((), (), s32[]{:S(2)}) async-start(), calls=%async_computation.18 | async-start | bytes 2654208 | tf_op jit(solution)/shard_map/reduce_scatter | solution.py:320
  640.0 173.0 %reduce-scatter.22.cloned.1.call-start = ((), (), s32[]{:S(2)}) async-start(), calls=%async_computation.22 | async-start | bytes 589824
  641.2 249.9 %all-reduce.12.cloned.1.call-start = ((), (), s32[]{:S(2)}) async-start(), calls=%async_computation.23 | async-start | bytes 9437184 | tf_op jit(solution)/shard_map/psum | solution.py:342
  679.5 216.8 %reduce-scatter.18.cloned.1.call-start = ((), (), s32[]{:S(2)}) async-start(), calls=%async_computation.20 | async-start | bytes 3538944 | tf_op jit(solution)/shard_map/reduce_scatter | solution.py:324
  686.6 209.7 %reduce-scatter.20.cloned.1.call-start = ((), (), s32[]{:S(2)}) async-start(), calls=%async_computation.21 | async-start | bytes 3538944 | tf_op jit(solution)/shard_map/reduce_scatter | solution.py:325
  718.9 95.1 %all-to-all-start.2 = ((bf16[4,2,36864]{2,1,0:T(2,128)(2,1)}), bf16[4,2,36864]{2,1,0:T(2,128)(2,1)}, u32[]{:S(2)}, u32[]{:S(2)}) async-start(bf16[4,2,36864]{2,1,0:T(2,128)(2,1)} %reshape.386), calls=%async_computation.4 | async-start | bytes 1179648 | tf_op jit(solution)/shard_map/all_to_all | solution.py:296
  731.1 90.1 %copy-start.4 = (bf16[768,2304]{1,0:T(8,128)(2,1)S(1)}, bf16[768,2304]{1,0:T(8,128)(2,1)}, u32[]{:S(2)}) copy-start(bf16[768,2304]{1,0:T(8,128)(2,1)} %all-gather.9.cloned.1.call-done) | copy-start | bytes 10616836
  731.1 90.1 %copy-start.27 = (f32[768]{0:T(1024)S(1)}, f32[768]{0:T(1024)}, u32[]{:S(2)}) copy-start(f32[768]{0:T(1024)} %copy-done.26) | copy-start | bytes 9220
  (39 other events, 176.3 us)
Sparse Core Ops, SparseCore 0:
  9.6 52.0 all-gather.8
  63.3 22.7 all-gather.10
  87.7 22.7 all-gather.14
  113.3 71.5 all-gather.12
  186.3 21.1 all-gather.16
  210.2 71.5 all-gather.18
  286.0 155.1 reduce-scatter.9
  445.8 155.9 reduce-scatter.11
  631.1 14.1 reduce-scatter.15
  648.1 28.3 reduce-scatter.13
  678.7 13.0 reduce-scatter.21
  696.4 119.0 all-reduce.11
  818.4 34.4 reduce-scatter.17
  855.6 34.6 reduce-scatter.19
